TPU v7x, 32 devices: a whole 2x2x4 slice. The times are simulated.
32 devices in a mesh: ens: 2 (over y), lat: 16 (over z, x, core).
Axes of the slice: x: 2, y: 2, z: 4, core: 2. Of those that a mesh axis runs over, the one named last changes fastest.
Arguments:
- field: bfloat16 [128, 1440, 384], P(('ens', 'lat')), parts along dimension 0, may hold values from -6 to 6
- norm_gain: float32 [384], replicated, may hold values from 0.1 to 1.9
- legendre_fwd: bfloat16 [256, 256, 64], P('lat'), as said below
- legendre_inv: bfloat16 [256, 256, 64], P('lat')
- degree_gain: float32 [256, 384], replicated, may hold values from 0.5 to 2
- mix_weight: bfloat16 [2, 384, 384], replicated, may hold values from -0.21875 to 0.21875
- mlp_gain: float32 [384], replicated, may hold values from 0.1 to 1.9
- up_weight: bfloat16 [384, 768], replicated, may hold values from -0.3125 to 0.3125
- up_bias: float32 [768], replicated, may hold values from -4 to 4
- down_weight: bfloat16 [768, 384], replicated, may hold values from -0.21875 to 0.21875
Outputs:
- result: bfloat16 [128, 1440, 384], P(('ens', 'lat')), parts along dimension 0
There are 2 independent parts, one for each index of `ens`. A program takes and returns all parts, laid end to end along the dimension named above; an argument that names none is the same for every part. Nothing has to cross between parts.
Inputs may be any that keep to these rules, and one draw needn't show every extreme that they name: legendre_inv holds orthonormal associated Legendre functions of degree l and order m (zero where l < m) at the grid's colatitudes, legendre_fwd the same times each row's quadrature weight.
All inputs are finite; a program needn't handle non-finite values.
Results may differ from a plain program's by a relative error of at most 0.009.
Values may be sent and summed in bfloat16 or wider, within the bound.
A program may use at most 64 MiB of HBM per device.

v0:
```python
import functools
import math

import jax
import jax.numpy as jnp
import numpy as np
from jax import lax
from jax.experimental import pallas as pl
from jax.experimental.pallas import tpu as pltpu
from jax.sharding import PartitionSpec as P

NLON = 1440
MMAX = 256


def dft_tables(nlon, modes):
    lon = jnp.arange(nlon, dtype=jnp.int32)
    wave = jnp.arange(modes, dtype=jnp.int32)
    phase = (wave[:, None] * lon[None, :] % nlon).astype(jnp.float32) * (2.0 * math.pi / nlon)
    scale = 2.0 * math.pi / nlon
    forward = jnp.stack([scale * jnp.cos(phase), -scale * jnp.sin(phase)], axis=1).reshape(
        2 * modes, nlon
    )
    weight = jnp.where(wave == 0, 1.0, 2.0).astype(jnp.float32)[:, None]
    inverse = jnp.stack([weight * jnp.cos(phase), -weight * jnp.sin(phase)], axis=1).reshape(
        2 * modes, nlon
    )
    return (forward.astype(jnp.bfloat16), inverse.T.astype(jnp.bfloat16))


def layer_norm(values, gain):
    values = values.astype(jnp.float32)
    center = values - jnp.mean(values, axis=-1, keepdims=True)
    spread = jnp.mean(center * center, axis=-1, keepdims=True)
    return center * lax.rsqrt(spread + 1e-05) * gain


def plain_shards(
    field,
    norm_gain,
    legendre_fwd,
    legendre_inv,
    degree_gain,
    mix_weight,
    mlp_gain,
    up_weight,
    up_bias,
    down_weight,
):
    lat_rows, nlon, chan = field.shape
    modes_here, degrees, all_lats = legendre_fwd.shape
    forward, inverse = dft_tables(NLON, MMAX)
    normed = layer_norm(field, norm_gain).astype(jnp.bfloat16)
    spectrum_lon = jnp.einsum("nk,jkc->jnc", forward, normed, preferred_element_type=jnp.float32)
    spectrum_lon = spectrum_lon.astype(jnp.bfloat16).reshape(lat_rows, MMAX, 2, chan)
    arrived = lax.all_to_all(spectrum_lon, "lat", split_axis=1, concat_axis=0, tiled=True)
    coeffs = jnp.einsum("mlj,jmrc->mlrc", legendre_fwd, arrived, preferred_element_type=jnp.float32)
    scaled = (
        (coeffs * degree_gain[None, :, None, :])
        .astype(jnp.bfloat16)
        .reshape(modes_here * degrees, 2 * chan)
    )
    block_w = jnp.concatenate(
        [
            jnp.concatenate([mix_weight[0], mix_weight[1]], 1),
            jnp.concatenate([-mix_weight[1], mix_weight[0]], 1),
        ],
        0,
    )
    mixed = (
        jnp.dot(scaled, block_w, preferred_element_type=jnp.float32)
        .astype(jnp.bfloat16)
        .reshape(modes_here, degrees, 2, chan)
    )
    synth_lon = jnp.einsum(
        "mlj,mlrc->jmrc", legendre_inv, mixed, preferred_element_type=jnp.float32
    ).astype(jnp.bfloat16)
    returned = lax.all_to_all(synth_lon, "lat", split_axis=0, concat_axis=1, tiled=True)
    rows, waves, parts, width = returned.shape
    flat = returned.reshape(rows, waves * parts, width)
    filtered = jnp.einsum("kn,jnc->jkc", inverse, flat, preferred_element_type=jnp.float32)
    inner = filtered + normed.astype(jnp.float32)
    post = layer_norm(inner, mlp_gain).astype(jnp.bfloat16).reshape(lat_rows * nlon, chan)
    hidden = jax.nn.gelu(
        jnp.dot(post, up_weight, preferred_element_type=jnp.float32) + up_bias
    ).astype(jnp.bfloat16)
    output = field.reshape(lat_rows * nlon, chan).astype(jnp.float32) + jnp.dot(
        hidden, down_weight, preferred_element_type=jnp.float32
    )
    return output.astype(jnp.bfloat16).reshape(lat_rows, nlon, chan)


CHUNKS = 2
TILE = 16
BF16, F32 = jnp.bfloat16, jnp.float32


def ordered_tables(nlon, modes, owners, chunks):
    here = modes // owners
    wave = np.arange(modes).reshape(owners, chunks, here // chunks).transpose(1, 0, 2).reshape(-1)
    phase = (wave[:, None] * np.arange(nlon)[None, :] % nlon) * (2.0 * np.pi / nlon)
    table = np.stack([np.cos(phase), -np.sin(phase)], axis=1)
    weight = np.where(wave == 0, 1.0, 2.0)[:, None, None]
    forward = (table * (2.0 * np.pi / nlon)).reshape(2 * modes, nlon)
    inverse = (table * weight).reshape(2 * modes, nlon)
    return (
        jnp.asarray(forward.astype(np.float32).astype(BF16)),
        jnp.asarray(np.ascontiguousarray(inverse.T).astype(np.float32).astype(BF16)),
    )


def normalize(values, gain):
    width = values.shape[-1]
    center = values - jnp.sum(values, axis=-1, keepdims=True) * (1.0 / width)
    spread = jnp.sum(center * center, axis=-1, keepdims=True) * (1.0 / width)
    return center * lax.rsqrt(spread + 1e-05) * gain


def kernel(
    n,
    step,
    norm_gain,
    mlp_gain,
    up_bias,
    field_h,
    forward_h,
    inverse_h,
    leg_fwd_h,
    leg_inv_h,
    degree_h,
    mix_h,
    up_h,
    down_h,
    out_h,
    field,
    normed,
    result,
    forward,
    inverse,
    leg_fwd,
    leg_inv,
    degree,
    mix,
    block_w,
    up,
    down,
    swap,
    sent,
    arrived,
    by_mode,
    synth,
    back,
    flat,
    in_sem,
    row_sem,
    out_sem,
    fs_sem,
    fr_sem,
    bs_sem,
    br_sem,
):
    rows, nlon, chan = field.shape
    chunks = sent.shape[0]
    modes_here, degrees, lats = leg_fwd.shape
    per_chunk = modes_here // chunks
    groups = lats // TILE
    owners = TILE // rows
    me = lax.axis_index("lat")

    row_copies = [
        pltpu.make_async_copy(field_h.at[r], field.at[r], row_sem.at[r]) for r in range(rows)
    ]
    loads = [
        pltpu.make_async_copy(a, b, in_sem.at[i])
        for i, (a, b) in enumerate(
            [
                (forward_h, forward),
                (leg_fwd_h, leg_fwd),
                (mix_h, mix),
                (degree_h, degree),
                (leg_inv_h, leg_inv),
                (inverse_h, inverse),
                (up_h, up),
                (down_h, down),
            ]
        )
    ]
    row_copies[0].start()
    loads[0].start()
    for copy in row_copies[1:] + loads[1:]:
        copy.start()

    def peer(t):
        offset = n // 2 + ((t + 1) // 2) * (2 * (t % 2) - 1)
        return (me + offset) % n

    barrier = pltpu.get_barrier_semaphore()

    def greet(t, carry):
        pl.semaphore_signal(
            barrier, inc=1, device_id={"lat": peer(t)}, device_id_type=pl.DeviceIdType.MESH
        )
        return carry

    lax.fori_loop(0, n - 1, greet, 0)

    def exchange(source, target, send_sem, recv_sem):
        def one(t, carry):
            to = peer(t)
            pltpu.make_async_remote_copy(
                src_ref=source(to),
                dst_ref=target(me),
                send_sem=send_sem,
                recv_sem=recv_sem,
                device_id={"lat": to},
                device_id_type=pl.DeviceIdType.MESH,
            ).start()
            return carry

        lax.fori_loop(0, n - 1, one, 0)
        pltpu.make_async_copy(source(me), target(me), recv_sem).start()

    def layer(r):
        def body(t, carry):
            at = pl.ds(pl.multiple_of(t * step, TILE), step)
            values = field[r, at, :].astype(F32)
            normed[r, at, :] = normalize(values, norm_gain[...]).astype(BF16)
            return carry

        lax.fori_loop(0, nlon // step, body, 0)

    for r in range(rows):
        row_copies[r].wait()
        layer(r)
        if r == 0:
            loads[0].wait()
        spec = jnp.dot(forward[...], normed[r], preferred_element_type=F32).astype(BF16)
        spec = spec.reshape(chunks, n, TILE, chan)
        for c in range(chunks):
            sent[c, :, r] = spec[c]
        if r == 0:
            pl.semaphore_wait(barrier, n - 1)
        exchange(
            lambda d: sent.at[0, d, r], lambda s: arrived.at[0, s, r], fs_sem.at[0], fr_sem.at[0]
        )
    for c in range(1, chunks):
        exchange(lambda d: sent.at[c, d], lambda s: arrived.at[c, s], fs_sem.at[c], fr_sem.at[c])

    for copy in loads[1:]:
        copy.wait()
    block_w[:chan, :chan] = mix[0]
    block_w[:chan, chan:] = mix[1]
    block_w[chan:, :chan] = -mix[1]
    block_w[chan:, chan:] = mix[0]
    a = lax.broadcasted_iota(jnp.int32, swap.shape, 0)
    b = lax.broadcasted_iota(jnp.int32, swap.shape, 1)
    swap[...] = ((a // TILE == b % TILE) & (a % TILE == b // TILE)).astype(F32).astype(BF16)

    def give(c, r):
        exchange(
            lambda d: back.at[c, r, d],
            lambda s: flat.at[r, c, s],
            bs_sem.at[c, r],
            br_sem.at[c, r],
        )

    for c in range(chunks):
        pltpu.make_async_copy(arrived.at[c], arrived.at[c], fr_sem.at[c]).wait()
        for g in range(groups):
            block = arrived[c, g * owners : (g + 1) * owners].reshape(TILE * TILE, chan)
            turned = jnp.dot(swap[...], block, preferred_element_type=F32).astype(BF16)
            by_mode[:, g * TILE : (g + 1) * TILE, :] = turned.reshape(TILE, TILE, chan)

        def one_mode(i, carry):
            m = c * per_chunk + i
            basis = leg_fwd[m]
            parts = [
                (
                    jnp.dot(basis, by_mode[2 * i + part], preferred_element_type=F32) * degree[...]
                ).astype(BF16)
                for part in range(2)
            ]
            scaled = jnp.concatenate(parts, axis=1)
            mixed = jnp.dot(scaled, block_w[...], preferred_element_type=F32).astype(BF16)
            rows_of = lax.dot_general(
                leg_inv[m], mixed, (((0,), (0,)), ((), ())), preferred_element_type=F32
            ).astype(BF16)
            synth[2 * i] = rows_of[:, :chan]
            synth[2 * i + 1] = rows_of[:, chan:]
            return carry

        lax.fori_loop(0, per_chunk, one_mode, 0)
        for g in range(groups):
            block = synth[:, g * TILE : (g + 1) * TILE, :].reshape(TILE * TILE, chan)
            turned = jnp.dot(swap[...], block, preferred_element_type=F32).astype(BF16)
            turned = turned.reshape(owners, rows, TILE, chan)
            for r in range(rows):
                back[c, r, g * owners : (g + 1) * owners] = turned[:, r]
        if c < chunks - 1:
            for r in range(rows // 2):
                give(c, r)
    for r in range(rows):
        for c in range(chunks):
            if c == chunks - 1 or r >= rows // 2:
                give(c, r)

    for r in range(rows):
        for c in range(chunks):
            pltpu.make_async_copy(flat.at[r, c], flat.at[r, c], br_sem.at[c, r]).wait()
        waves = flat[r].reshape(chunks * n * TILE, chan)

        def finish(t, carry):
            at = pl.ds(pl.multiple_of(t * step, TILE), step)
            inner = jnp.dot(inverse[at, :], waves, preferred_element_type=F32)
            inner = inner + normed[r, at, :].astype(F32)
            post = normalize(inner, mlp_gain[...]).astype(BF16)
            hidden = jnp.dot(post, up[...], preferred_element_type=F32) + up_bias[...]
            hidden = jax.nn.gelu(hidden).astype(BF16)
            total = field[r, at, :].astype(F32) + jnp.dot(
                hidden, down[...], preferred_element_type=F32
            )
            result[r, at, :] = total.astype(BF16)
            return carry

        lax.fori_loop(0, nlon // step, finish, 0)
        pltpu.make_async_copy(result.at[r], out_h.at[r], out_sem.at[r]).start()

    for c in range(chunks):
        piece = sent.at[c, pl.ds(0, n - 1)]
        pltpu.make_async_copy(piece, piece, fs_sem.at[c]).wait()
        for r in range(rows):
            piece = back.at[c, r, pl.ds(0, n - 1)]
            pltpu.make_async_copy(piece, piece, bs_sem.at[c, r]).wait()
    for r in range(rows):
        pltpu.make_async_copy(result.at[r], out_h.at[r], out_sem.at[r]).wait()


def shards(
    n,
    field,
    norm_gain,
    legendre_fwd,
    legendre_inv,
    degree_gain,
    mix_weight,
    mlp_gain,
    up_weight,
    up_bias,
    down_weight,
):
    args = (field, norm_gain, legendre_fwd, legendre_inv, degree_gain, mix_weight)
    args = args + (mlp_gain, up_weight, up_bias, down_weight)
    rows, nlon, chan = field.shape
    modes_here, degrees, lats = legendre_fwd.shape
    width = up_weight.shape[1]
    if 2 * modes_here != CHUNKS * TILE or TILE % rows or lats % TILE:
        return plain_shards(*args)
    forward, inverse = ordered_tables(nlon, modes_here * n, n, CHUNKS)
    step = nlon // 6 if nlon % (6 * TILE) == 0 else nlon
    any_spec = pl.BlockSpec(memory_space=pl.ANY)
    vmem = pl.BlockSpec(memory_space=pltpu.VMEM)
    dma = pltpu.SemaphoreType.DMA
    return pl.pallas_call(
        functools.partial(kernel, n, step),
        out_shape=jax.ShapeDtypeStruct(field.shape, field.dtype),
        in_specs=[vmem] * 3 + [any_spec] * 9,
        out_specs=any_spec,
        scratch_shapes=[
            pltpu.VMEM((rows, nlon, chan), BF16),
            pltpu.VMEM((rows, nlon, chan), BF16),
            pltpu.VMEM((rows, nlon, chan), BF16),
            pltpu.VMEM(forward.shape, BF16),
            pltpu.VMEM(inverse.shape, BF16),
            pltpu.VMEM(legendre_fwd.shape, BF16),
            pltpu.VMEM(legendre_inv.shape, BF16),
            pltpu.VMEM(degree_gain.shape, F32),
            pltpu.VMEM(mix_weight.shape, BF16),
            pltpu.VMEM((2 * chan, 2 * chan), BF16),
            pltpu.VMEM(up_weight.shape, BF16),
            pltpu.VMEM(down_weight.shape, BF16),
            pltpu.VMEM((TILE * TILE, TILE * TILE), BF16),
            pltpu.VMEM((CHUNKS, n, rows, TILE, chan), BF16),
            pltpu.VMEM((CHUNKS, n, rows, TILE, chan), BF16),
            pltpu.VMEM((TILE, lats, chan), BF16),
            pltpu.VMEM((TILE, lats, chan), BF16),
            pltpu.VMEM((CHUNKS, rows, n, TILE, chan), BF16),
            pltpu.VMEM((rows, CHUNKS, n, TILE, chan), BF16),
            dma((8,)),
            dma((rows,)),
            dma((rows,)),
            dma((CHUNKS,)),
            dma((CHUNKS,)),
            dma((CHUNKS, rows)),
            dma((CHUNKS, rows)),
        ],
        compiler_params=pltpu.CompilerParams(
            collective_id=0, has_side_effects=True, vmem_limit_bytes=56 << 20
        ),
    )(
        norm_gain.reshape(1, chan),
        mlp_gain.reshape(1, chan),
        up_bias.reshape(1, width),
        field,
        forward,
        inverse,
        legendre_fwd,
        legendre_inv,
        degree_gain,
        mix_weight,
        up_weight,
        down_weight,
    )


def solution(mesh):
    return jax.shard_map(
        functools.partial(shards, mesh.shape["lat"]),
        mesh=mesh,
        in_specs=(
            P(("ens", "lat"), None, None),
            P(),
            P("lat", None, None),
            P("lat", None, None),
            P(),
            P(),
            P(),
            P(),
            P(),
            P(),
        ),
        out_specs=P(("ens", "lat"), None, None),
        check_vma=False,
    )
```

profile of v0, /device:TPU:0, one launch (start us, length us, event | category | flops | bytes accessed | tf_op | source)
XLA Modules:
  0.0 101.6 jit_solution(16136444038630838779)
XLA Ops:
  0.0 1.2 %reshape.9.norm_gain = f32[1,384]{1,0:T(1,128)} reshape(f32[384]{0:T(512)} %param.13) | data formatting | bytes 3072 | tf_op jit(solution)/shard_map/reshape | solution.py:400
  1.2 1.3 %reshape.10.mlp_gain = f32[1,384]{1,0:T(1,128)} reshape(f32[384]{0:T(512)} %param.18) | data formatting | bytes 3072 | tf_op jit(solution)/shard_map/reshape | solution.py:401
  2.5 1.3 %reshape.11.up_bias = f32[1,768]{1,0:T(1,128)} reshape(f32[768]{0:T(1024)} %param.20) | data formatting | bytes 6144 | tf_op jit(solution)/shard_map/reshape | solution.py:402
  3.8 2.4 %copy.13.leg_fwd_h = bf16[16,256,64]{2,1,0:T(8,128)(2,1)} copy(bf16[16,256,64]{1,2,0:T(8,128)(2,1)} %param.14) | data formatting | bytes 1048576 | tf_op args[2]
  6.2 2.3 %copy.14.leg_inv_h = bf16[16,256,64]{2,1,0:T(8,128)(2,1)} copy(bf16[16,256,64]{1,2,0:T(8,128)(2,1)} %param.15) | data formatting | bytes 1048576 | tf_op args[3]
  8.5 88.3 %shard_map.118 = bf16[4,1440,384]{2,1,0:T(8,128)(2,1)} custom-call(f32[1,384]{1,0:T(1,128)} %reshape.9.norm_gain, f32[1,384]{1,0:T(1,128)} %reshape.10.mlp_gain, f32[1,768]{1,0:T(1,128)} %reshape.11.up_bias, bf16[4,1440,384]{2,1,0:T(8,128)(2,1)} %field_h.1, bf16[512,1440]{1,0:T(8,128)(2,1)} %constant.4.clone.forward_h, ...), custom_call_target="tpu_custom_call" | custom-call | tf_op jit(solution)/shard_map/pallas_call | solution.py:363
  96.8 4.8 %copy.16 = bf16[4,1440,384]{2,1,0:T(8,128)(2,1)} copy(bf16[4,1440,384]{2,1,0:T(8,128)(2,1)} %shard_map.118) | data formatting | bytes 8847360
where the time goes:
time: 102 us
  Pallas kernels  88.3 us (87%)
  local copies, waits for them, and re-layouts  13.3 us (13%)
    pallas_call x1, Pallas kernels, shards(): pl.pallas_call(functools.partial(kernel, n, step), out_shape=jax.ShapeDty...  88.3 us
    unnamed x3, local copies, waits for them, and re-layouts  9.49 us

commit v1 on v0

--- a/solution.py
+++ b/solution.py
@@ -91,6 +91,10 @@
 
 
 CHUNKS = 2
+GATE1 = True
+GATE2 = True
+OUTV = False
+UNROLL_LN, UNROLL_FIN, UNROLL_MODE = 3, 6, 2
 TILE = 16
 BF16, F32 = jnp.bfloat16, jnp.float32
 
@@ -161,11 +165,12 @@
 ):
     rows, nlon, chan = field.shape
     chunks = sent.shape[0]
-    modes_here, degrees, lats = leg_fwd.shape
+    modes_here, lats, degrees = leg_fwd.shape
     per_chunk = modes_here // chunks
     groups = lats // TILE
     owners = TILE // rows
     me = lax.axis_index("lat")
+    half = forward.shape[0] // chunks
 
     row_copies = [
         pltpu.make_async_copy(field_h.at[r], field.at[r], row_sem.at[r]) for r in range(rows)
@@ -174,7 +179,8 @@
         pltpu.make_async_copy(a, b, in_sem.at[i])
         for i, (a, b) in enumerate(
             [
-                (forward_h, forward),
+                (forward_h.at[:half], forward.at[:half]),
+                (forward_h.at[half:], forward.at[half:]),
                 (leg_fwd_h, leg_fwd),
                 (mix_h, mix),
                 (degree_h, degree),
@@ -187,8 +193,6 @@
     ]
     row_copies[0].start()
     loads[0].start()
-    for copy in row_copies[1:] + loads[1:]:
-        copy.start()
 
     def peer(t):
         offset = n // 2 + ((t + 1) // 2) * (2 * (t % 2) - 1)
@@ -220,6 +224,9 @@
         lax.fori_loop(0, n - 1, one, 0)
         pltpu.make_async_copy(source(me), target(me), recv_sem).start()
 
+    def gone(piece, sem):
+        pltpu.make_async_copy(piece, piece, sem).wait()
+
     def layer(r):
         def body(t, carry):
             at = pl.ds(pl.multiple_of(t * step, TILE), step)
@@ -227,27 +234,37 @@
             normed[r, at, :] = normalize(values, norm_gain[...]).astype(BF16)
             return carry
 
-        lax.fori_loop(0, nlon // step, body, 0)
+        lax.fori_loop(0, nlon // step, body, 0, unroll=UNROLL_LN)
+
+    def spectrum(c, r):
+        spec = jnp.dot(
+            forward[c * half : (c + 1) * half, :], normed[r], preferred_element_type=F32
+        )
+        sent[c, :, r] = spec.astype(BF16).reshape(n, TILE, chan)
 
     for r in range(rows):
         row_copies[r].wait()
+        if r == 0:
+            for copy in row_copies[1:] + loads[1:]:
+                copy.start()
         layer(r)
         if r == 0:
             loads[0].wait()
-        spec = jnp.dot(forward[...], normed[r], preferred_element_type=F32).astype(BF16)
-        spec = spec.reshape(chunks, n, TILE, chan)
-        for c in range(chunks):
-            sent[c, :, r] = spec[c]
+        spectrum(0, r)
         if r == 0:
             pl.semaphore_wait(barrier, n - 1)
         exchange(
             lambda d: sent.at[0, d, r], lambda s: arrived.at[0, s, r], fs_sem.at[0], fr_sem.at[0]
         )
-    for c in range(1, chunks):
-        exchange(lambda d: sent.at[c, d], lambda s: arrived.at[c, s], fs_sem.at[c], fr_sem.at[c])
-
     for copy in loads[1:]:
         copy.wait()
+    for c in range(1, chunks):
+        for r in range(rows):
+            spectrum(c, r)
+        if GATE1:
+            gone(sent.at[c - 1, pl.ds(0, n - 1)], fs_sem.at[c - 1])
+        exchange(lambda d: sent.at[c, d], lambda s: arrived.at[c, s], fs_sem.at[c], fr_sem.at[c])
+
     block_w[:chan, :chan] = mix[0]
     block_w[:chan, chan:] = mix[1]
     block_w[chan:, :chan] = -mix[1]
@@ -273,23 +290,19 @@
 
         def one_mode(i, carry):
             m = c * per_chunk + i
-            basis = leg_fwd[m]
-            parts = [
-                (
-                    jnp.dot(basis, by_mode[2 * i + part], preferred_element_type=F32) * degree[...]
-                ).astype(BF16)
-                for part in range(2)
-            ]
-            scaled = jnp.concatenate(parts, axis=1)
+            both = jnp.concatenate([by_mode[2 * i], by_mode[2 * i + 1]], axis=1)
+            coeffs = lax.dot_general(
+                leg_fwd[m], both, (((0,), (0,)), ((), ())), preferred_element_type=F32
+            )
+            parts = [coeffs[:, :chan] * degree[...], coeffs[:, chan:] * degree[...]]
+            scaled = jnp.concatenate(parts, axis=1).astype(BF16)
             mixed = jnp.dot(scaled, block_w[...], preferred_element_type=F32).astype(BF16)
-            rows_of = lax.dot_general(
-                leg_inv[m], mixed, (((0,), (0,)), ((), ())), preferred_element_type=F32
-            ).astype(BF16)
+            rows_of = jnp.dot(leg_inv[m], mixed, preferred_element_type=F32).astype(BF16)
             synth[2 * i] = rows_of[:, :chan]
             synth[2 * i + 1] = rows_of[:, chan:]
             return carry
 
-        lax.fori_loop(0, per_chunk, one_mode, 0)
+        lax.fori_loop(0, per_chunk, one_mode, 0, unroll=UNROLL_MODE)
         for g in range(groups):
             block = synth[:, g * TILE : (g + 1) * TILE, :].reshape(TILE * TILE, chan)
             turned = jnp.dot(swap[...], block, preferred_element_type=F32).astype(BF16)
@@ -297,6 +310,8 @@
             for r in range(rows):
                 back[c, r, g * owners : (g + 1) * owners] = turned[:, r]
         if c < chunks - 1:
+            if GATE2:
+                gone(sent.at[c + 1, pl.ds(0, n - 1)], fs_sem.at[c + 1])
             for r in range(rows // 2):
                 give(c, r)
     for r in range(rows):
@@ -304,13 +319,13 @@
             if c == chunks - 1 or r >= rows // 2:
                 give(c, r)
 
-    for r in range(rows):
+    def finish_row(r, carry):
         for c in range(chunks):
-            pltpu.make_async_copy(flat.at[r, c], flat.at[r, c], br_sem.at[c, r]).wait()
-        waves = flat[r].reshape(chunks * n * TILE, chan)
+            gone(flat.at[r, c], br_sem.at[c, r])
 
         def finish(t, carry):
             at = pl.ds(pl.multiple_of(t * step, TILE), step)
+            waves = flat[r].reshape(chunks * n * TILE, chan)
             inner = jnp.dot(inverse[at, :], waves, preferred_element_type=F32)
             inner = inner + normed[r, at, :].astype(F32)
             post = normalize(inner, mlp_gain[...]).astype(BF16)
@@ -322,17 +337,21 @@
             result[r, at, :] = total.astype(BF16)
             return carry
 
-        lax.fori_loop(0, nlon // step, finish, 0)
-        pltpu.make_async_copy(result.at[r], out_h.at[r], out_sem.at[r]).start()
+        lax.fori_loop(0, nlon // step, finish, 0, unroll=UNROLL_FIN)
+        if not OUTV:
+            pltpu.make_async_copy(result.at[r], out_h.at[r], out_sem.at[r]).start()
+        return carry
+
+    lax.fori_loop(0, rows, finish_row, 0)
 
     for c in range(chunks):
-        piece = sent.at[c, pl.ds(0, n - 1)]
-        pltpu.make_async_copy(piece, piece, fs_sem.at[c]).wait()
+        if not (GATE1 if c < chunks - 1 else GATE2):
+            gone(sent.at[c, pl.ds(0, n - 1)], fs_sem.at[c])
         for r in range(rows):
-            piece = back.at[c, r, pl.ds(0, n - 1)]
-            pltpu.make_async_copy(piece, piece, bs_sem.at[c, r]).wait()
-    for r in range(rows):
-        pltpu.make_async_copy(result.at[r], out_h.at[r], out_sem.at[r]).wait()
+            gone(back.at[c, r, pl.ds(0, n - 1)], bs_sem.at[c, r])
+    if not OUTV:
+        for r in range(rows):
+            pltpu.make_async_copy(result.at[r], out_h.at[r], out_sem.at[r]).wait()
 
 
 def shards(
@@ -352,7 +371,6 @@
     args = args + (mlp_gain, up_weight, up_bias, down_weight)
     rows, nlon, chan = field.shape
     modes_here, degrees, lats = legendre_fwd.shape
-    width = up_weight.shape[1]
     if 2 * modes_here != CHUNKS * TILE or TILE % rows or lats % TILE:
         return plain_shards(*args)
     forward, inverse = ordered_tables(nlon, modes_here * n, n, CHUNKS)
@@ -371,8 +389,8 @@
             pltpu.VMEM((rows, nlon, chan), BF16),
             pltpu.VMEM(forward.shape, BF16),
             pltpu.VMEM(inverse.shape, BF16),
-            pltpu.VMEM(legendre_fwd.shape, BF16),
-            pltpu.VMEM(legendre_inv.shape, BF16),
+            pltpu.VMEM((modes_here, lats, degrees), BF16),
+            pltpu.VMEM((modes_here, lats, degrees), BF16),
             pltpu.VMEM(degree_gain.shape, F32),
             pltpu.VMEM(mix_weight.shape, BF16),
             pltpu.VMEM((2 * chan, 2 * chan), BF16),
@@ -385,7 +403,7 @@
             pltpu.VMEM((TILE, lats, chan), BF16),
             pltpu.VMEM((CHUNKS, rows, n, TILE, chan), BF16),
             pltpu.VMEM((rows, CHUNKS, n, TILE, chan), BF16),
-            dma((8,)),
+            dma((9,)),
             dma((rows,)),
             dma((rows,)),
             dma((CHUNKS,)),
@@ -397,14 +415,14 @@
             collective_id=0, has_side_effects=True, vmem_limit_bytes=56 << 20
         ),
     )(
-        norm_gain.reshape(1, chan),
-        mlp_gain.reshape(1, chan),
-        up_bias.reshape(1, width),
+        norm_gain,
+        mlp_gain,
+        up_bias,
         field,
         forward,
         inverse,
-        legendre_fwd,
-        legendre_inv,
+        jnp.swapaxes(legendre_fwd, 1, 2),
+        jnp.swapaxes(legendre_inv, 1, 2),
         degree_gain,
         mix_weight,
         up_weight,

time: 102 us -> 89.9 us (0.88)
  local copies, waits for them, and re-layouts: 13.3 us -> 4.78 us
  Pallas kernels: 88.3 us -> 84.9 us
    unnamed x3 -> x1, local copies, waits for them, and re-layouts: 9.49 us -> 4.78 us
    reshape x3 -> x0, local copies, waits for them, and re-layouts: 3.8 us -> none  [the longest x1 1.28 us: shards(): up_bias.reshape(1, width)]
    pallas_call x1, Pallas kernels: 88.3 us -> 84.9 us  [shards(): pl.pallas_call(functools.partial(kernel, n, step), out_shape=jax.ShapeDty...]
where the time goes in v1:
time: 89.9 us; the launch traced here: 89.7 us
  Pallas kernels  84.9 us (94%)
  local copies, waits for them, and re-layouts  4.78 us (5%)
    pallas_call x1, Pallas kernels, shards(): pl.pallas_call(functools.partial(kernel, n, step), out_shape=jax.ShapeDty...  84.9 us
    unnamed x1, local copies, waits for them, and re-layouts  4.78 us

profile of v1, /device:TPU:0, one launch (start us, length us, event | category | flops | bytes accessed | tf_op | source)
XLA Modules:
  0.0 89.7 jit_solution(13082535983344495597)
XLA Ops:
  0.0 84.9 %shard_map.118 = bf16[4,1440,384]{2,1,0:T(8,128)(2,1)} custom-call(f32[384]{0:T(512)} %norm_gain.1, f32[384]{0:T(512)} %mlp_gain.1, f32[768]{0:T(1024)} %up_bias.1, bf16[4,1440,384]{2,1,0:T(8,128)(2,1)} %field_h.1, bf16[512,1440]{1,0:T(8,128)(2,1)} %constant.4.clone.forward_h, bf16[1440,512]{1,0:T(8,128)(2,1)} %constant.5.clone.inverse_h, ...), custom_call_target="tpu_custom_call" | custom-call | tf_op jit(solution)/shard_map/pallas_call | solution.py:381
  84.9 4.8 %copy.14 = bf16[4,1440,384]{2,1,0:T(8,128)(2,1)} copy(bf16[4,1440,384]{2,1,0:T(8,128)(2,1)} %shard_map.118) | data formatting | bytes 8847360
